TPU v7x, 768 devices: a whole 4x8x12 slice. The times are simulated.
768 devices in a mesh: dp: 64 (over y, z_lo, core), resp: 12 (over x, z_hi).
Axes of the slice: x: 4, y: 8, z: 12 (z_hi: 3, z_lo: 4; z = z_hi * 4 + z_lo), core: 2. Of those that a mesh axis runs over, the one named last changes fastest.
Arguments:
- queries: bfloat16 [768, 128, 2560], P(('dp', 'resp')), may hold values from -6 to 6
- resp_keys: bfloat16 [768, 128, 512], P(('dp', 'resp')), may hold values from -6 to 6
- resp_values: bfloat16 [768, 128, 512], P(('dp', 'resp')), may hold values from -6 to 6
- grad_out: bfloat16 [768, 128, 2560], P(('dp', 'resp')), may hold values from -6 to 6
- forward_out: bfloat16 [768, 128, 2560], P(('dp', 'resp')), may hold values from -2 to 2
- log_norm: float32 [768, 128, 20], P(('dp', 'resp')), may hold values from 5 to 8
- prompt_keys: bfloat16 [12, 1024, 512], P('resp', 'dp'), may hold values from -6 to 6
- prompt_values: bfloat16 [12, 1024, 512], P('resp', 'dp'), may hold values from -6 to 6
- resp_len: int32 [768], P(('dp', 'resp')), may hold values from 1 to 128, as said below
- seen_blocks: int32 [768], P(('dp', 'resp')), may hold values from 1 to 48, as said below
Outputs:
- grad_queries: bfloat16 [768, 128, 2560], P(('dp', 'resp'))
- grad_resp_keys: bfloat16 [768, 128, 512], P(('dp', 'resp'))
- grad_resp_values: bfloat16 [768, 128, 512], P(('dp', 'resp'))
- grad_prompt_keys: float32 [12, 1024, 512], P('resp', 'dp')
- grad_prompt_values: float32 [12, 1024, 512], P('resp', 'dp')
Inputs may be any that keep to these rules, and one draw needn't show every extreme that they name: `resp_len`: some response has all 128 tokens live. `seen_blocks`: some response reads all 48 blocks.
All inputs are finite; a program needn't handle non-finite values.
Results may differ from a plain program's by a relative error of at most 0.009.
Values may be sent and summed in bfloat16 or wider, within the bound.
A program may use at most 32 MiB of HBM per device.

v0:
```python
import jax
import jax.numpy as jnp
from jax import lax
from jax.sharding import PartitionSpec as P

HQ = 20
HK = 4
DH = 128
GROUP = 4
PB = 16


def shortened(array):
    return jax.tree.map(lambda a: a.astype(jnp.bfloat16) if a.dtype == jnp.float32 else a, array)


def from_partner(array, axis, bit):
    return lax.ppermute(array, axis, [(i, i ^ 1 << bit) for i in range(lax.axis_size(axis))])


def shifted(value, axis, steps):
    count = lax.axis_size(axis)
    pairs = [(source, (source + steps) % count) for source in range(count)]
    return lax.ppermute(value, axis, pairs)


def pair_grads(q4, do4, lse, delta, keys, vals, visible, scale):
    scores = jnp.einsum("tgrd,kgd->tgrk", q4, keys, preferred_element_type=jnp.float32) * scale
    probs = jnp.where(visible[:, None, None, :], jnp.exp(scores - lse[..., None]), 0.0)
    dprob = jnp.einsum("tgrd,kgd->tgrk", do4, vals, preferred_element_type=jnp.float32)
    dscore = probs * (dprob - delta[..., None])
    probs16 = probs.astype(jnp.bfloat16)
    dscore16 = dscore.astype(jnp.bfloat16)
    grad_v = jnp.einsum("tgrk,tgrd->kgd", probs16, do4, preferred_element_type=jnp.float32)
    grad_k = jnp.einsum("tgrk,tgrd->kgd", dscore16, q4, preferred_element_type=jnp.float32) * scale
    grad_q = (
        jnp.einsum("tgrk,kgd->tgrd", dscore16, keys, preferred_element_type=jnp.float32) * scale
    )
    return (grad_q, grad_k, grad_v)


def shards(
    queries,
    resp_keys,
    resp_values,
    grad_out,
    forward_out,
    log_norm,
    prompt_keys,
    prompt_values,
    resp_len,
    seen_blocks,
):
    rows = queries.shape[1]
    width = resp_keys.shape[2]
    ratio = HQ // HK
    scale = 1.0 / DH**0.5
    bits = GROUP.bit_length() - 1
    q4 = queries[0].reshape(rows, HK, ratio, DH)
    do4 = grad_out[0].reshape(rows, HK, ratio, DH)
    o4 = forward_out[0].reshape(rows, HK, ratio, DH)
    delta = jnp.sum(do4.astype(jnp.float32) * o4.astype(jnp.float32), axis=-1)
    lse = log_norm[0].reshape(rows, HK, ratio)
    length = resp_len[0]
    seen = seen_blocks[0]
    tpos = jnp.arange(rows, dtype=jnp.int32)
    live = tpos < length
    my_row = lax.axis_index("dp") % GROUP
    column = lax.axis_index("resp")
    loop_size = lax.axis_size("resp")
    self_ok = live[:, None] & (tpos[None, :] <= tpos[:, None])
    gq_self, gk_self, gv_self = pair_grads(
        q4,
        do4,
        lse,
        delta,
        resp_keys[0].reshape(rows, HK, DH),
        resp_values[0].reshape(rows, HK, DH),
        self_ok,
        scale,
    )

    def collect(pair):
        for bit in range(bits):
            other = jax.tree.map(
                lambda part, own: part.astype(own.dtype),
                from_partner(shortened(pair), "dp", bit),
                pair,
            )
            upper = my_row >> bit & 1 == 1
            pair = tuple(
                (
                    jnp.where(
                        upper,
                        jnp.concatenate([theirs, mine], 0),
                        jnp.concatenate([mine, theirs], 0),
                    )
                    for mine, theirs in zip(pair, other)
                )
            )
        return pair

    def return_sum(pair):
        for bit in reversed(range(bits)):
            half = pair[0].shape[0] // 2
            upper = my_row >> bit & 1 == 1
            lower_part = tuple((piece[:half] for piece in pair))
            upper_part = tuple((piece[half:] for piece in pair))
            sending = tuple(
                (jnp.where(upper, low, high) for low, high in zip(lower_part, upper_part))
            )
            received = from_partner(sending, "dp", bit)
            pair = tuple(
                (
                    jnp.where(upper, high, low) + got
                    for low, high, got in zip(lower_part, upper_part, received)
                )
            )
        return pair

    def visit(grad_q, bundle_k, bundle_v, col):
        count = bundle_k.shape[0]
        block_of = col * GROUP + jnp.arange(count, dtype=jnp.int32) // PB
        visible = live[:, None] & (block_of < seen)[None, :]

        def compute(operand):
            gq, gk, gv = pair_grads(
                q4,
                do4,
                lse,
                delta,
                bundle_k.reshape(count, HK, DH),
                bundle_v.reshape(count, HK, DH),
                visible,
                scale,
            )
            return (grad_q + gq, gk.reshape(count, width), gv.reshape(count, width))

        def skip(operand):
            empty = jnp.zeros((count, width), jnp.float32)
            return (grad_q, empty, empty)

        return lax.cond(col * GROUP < seen, compute, skip, None)

    def move_blocks(pair):
        return shifted((pair[0], pair[1]), "resp", 1)

    def move_sums(pair):
        return shifted((pair[0], pair[1]), "resp", 1)

    start_q = jnp.zeros((rows, HK, ratio, DH), jnp.float32)
    own_k = prompt_keys[0]
    own_v = prompt_values[0]
    zero = jnp.zeros(own_k.shape, jnp.float32)

    def step(index, carry):
        grad_q, blk_k, blk_v, sum_k, sum_v = carry
        col = (column - index) % loop_size
        bundle_k, bundle_v = collect((blk_k, blk_v))
        grad_q, part_k, part_v = visit(grad_q, bundle_k, bundle_v, col)
        mine_k, mine_v = return_sum((part_k, part_v))
        blk_k, blk_v = move_blocks((blk_k, blk_v))
        sum_k, sum_v = move_sums((sum_k + mine_k, sum_v + mine_v))
        return (grad_q, blk_k, blk_v, sum_k, sum_v)

    grad_q, blk_k, blk_v, sum_k, sum_v = lax.fori_loop(
        0, loop_size, step, (start_q, own_k, own_v, zero, zero)
    )
    grad_queries = (grad_q + gq_self).reshape(1, rows, HQ * DH).astype(jnp.bfloat16)
    grad_rk = gk_self.reshape(1, rows, width).astype(jnp.bfloat16)
    grad_rv = gv_self.reshape(1, rows, width).astype(jnp.bfloat16)
    return (
        grad_queries,
        grad_rk,
        grad_rv,
        sum_k.reshape(1, -1, width),
        sum_v.reshape(1, -1, width),
    )


def solution(mesh):
    return jax.shard_map(
        shards,
        mesh=mesh,
        in_specs=(
            P(("dp", "resp"), None, None),
            P(("dp", "resp"), None, None),
            P(("dp", "resp"), None, None),
            P(("dp", "resp"), None, None),
            P(("dp", "resp"), None, None),
            P(("dp", "resp"), None, None),
            P("resp", "dp", None),
            P("resp", "dp", None),
            P(("dp", "resp")),
            P(("dp", "resp")),
        ),
        out_specs=(
            P(("dp", "resp"), None, None),
            P(("dp", "resp"), None, None),
            P(("dp", "resp"), None, None),
            P("resp", "dp", None),
            P("resp", "dp", None),
        ),
        check_vma=False,
    )
```

profile of v0, /device:TPU:144, one launch (start us, length us, event | category | flops | bytes accessed | tf_op | source)
XLA Modules:
  0.0 678.8 jit_solution(13964926420083297038)
XLA Ops:
  13.2 660.2 %while.28 = (s32[]{:T(128)}, f32[128,4,5,128]{3,0,2,1:T(8,128)S(1)}, bf16[16,512]{1,0:T(8,128)(2,1)S(1)}, bf16[16,512]{1,0:T(8,128)(2,1)S(1)}, f32[16,512]{1,0:T...) while((s32[]{:T(128)}, ...), condition=%wide.region_4.5_spmd.clone, body=%wide.region_1.4_spmd.clone.sunk | while | flops 212607760 | bytes 14019364 | solution.py:166
  42.7 10.6 %collective-permute-start.11 = (f32[16,512]{1,0:T(8,128)S(1)}, f32[16,512]{1,0:T(8,128)S(1)}, u32[]{:S(2)}, u32[]{:S(2)}) collective-permute-start(f32[16,512]{1,0:T(8,128)S(1)} %add_add_fusion.5), channel_id=1, source_target_pairs={{0,1},{1,2},{2,3},{3,4},{4,5},{5,6},{6,7},{7,8},{8,9},{9,10},{10,1... | collective-permute-start | bytes 98312 | tf_op jit(solution)/shard_map/while/body/eval_jaxpr/ppermute | solution.py:24
  53.4 5.9 collective-permute-start.8
  61.2 7.0 %collective-permute-start.5 = (bf16[16,512]{1,0:T(8,128)(2,1)S(1)}, bf16[16,512]{1,0:T(8,128)(2,1)S(1)}, u32[]{:S(2)}, u32[]{:S(2)}) collective-permute-start(bf16[16,512]{1,0:T(8,128)(2,1)S(1)} %copy.126), channel_id=1, source_target_pairs={{0,1},{1,2},{2,3},{3,4},{4,5},{5,6},{6,7},{7,8},{8,9},{9,10},{10,1... | collective-permute-start | bytes 49160 | tf_op jit(solution)/shard_map/while/body/eval_jaxpr/ppermute | solution.py:24
  100.5 5.7 collective-permute-start.11
  113.2 7.1 %collective-permute-start.5 = (bf16[16,512]{1,0:T(8,128)(2,1)S(1)}, bf16[16,512]{1,0:T(8,128)(2,1)S(1)}, u32[]{:S(2)}, u32[]{:S(2)}) collective-permute-start(bf16[16,512]{1,0:T(8,128)(2,1)S(1)} %copy.126), channel_id=1, source_target_pairs={{0,1},{1,2},{2,3},{3,4},{4,5},{5,6},{6,7},{7,8},{8,9},{9,10},{10,1... | collective-permute-start | bytes 49160 | tf_op jit(solution)/shard_map/while/body/eval_jaxpr/ppermute | solution.py:24
  154.9 8.6 %collective-permute-start.8 = (f32[16,512]{1,0:T(8,128)S(1)}, f32[16,512]{1,0:T(8,128)S(1)}, u32[]{:S(2)}, u32[]{:S(2)}) collective-permute-start(f32[16,512]{1,0:T(8,128)S(1)} %add_add_fusion.4), channel_id=1, source_target_pairs={{0,1},{1,2},{2,3},{3,4},{4,5},{5,6},{6,7},{7,8},{8,9},{9,10},{10,1... | collective-permute-start | bytes 98312 | tf_op jit(solution)/shard_map/while/body/eval_jaxpr/ppermute | solution.py:24
  163.5 6.6 collective-permute-start.4
  175.3 6.5 collective-permute-done.5
  211.8 7.9 %collective-permute-start.8 = (f32[16,512]{1,0:T(8,128)S(1)}, f32[16,512]{1,0:T(8,128)S(1)}, u32[]{:S(2)}, u32[]{:S(2)}) collective-permute-start(f32[16,512]{1,0:T(8,128)S(1)} %add_add_fusion.4), channel_id=1, source_target_pairs={{0,1},{1,2},{2,3},{3,4},{4,5},{5,6},{6,7},{7,8},{8,9},{9,10},{10,1... | collective-permute-start | bytes 98312 | tf_op jit(solution)/shard_map/while/body/eval_jaxpr/ppermute | solution.py:24
  219.7 4.9 collective-permute-start.4
  226.5 4.8 collective-permute-done.4
  231.4 4.9 collective-permute-done.5
  266.1 6.4 collective-permute-start.8
  275.4 4.3 collective-permute-start.5
  279.8 5.0 collective-permute-done.4
  317.9 5.1 collective-permute-start.8
  323.0 7.7 %collective-permute-start.4 = (bf16[16,512]{1,0:T(8,128)(2,1)S(1)}, bf16[16,512]{1,0:T(8,128)(2,1)S(1)}, u32[]{:S(2)}, u32[]{:S(2)}) collective-permute-start(bf16[16,512]{1,0:T(8,128)(2,1)S(1)} %copy.125), channel_id=1, source_target_pairs={{0,1},{1,2},{2,3},{3,4},{4,5},{5,6},{6,7},{7,8},{8,9},{9,10},{10,1... | collective-permute-start | bytes 49160 | tf_op jit(solution)/shard_map/while/body/eval_jaxpr/ppermute | solution.py:24
  335.2 7.2 %collective-permute-done.5 = bf16[16,512]{1,0:T(8,128)(2,1)S(1)} collective-permute-done((bf16[16,512]{1,0:T(8,128)(2,1)S(1)}, bf16[16,512]{1,0:T(8,128)(2,1)S(1)}, u32[]{:S(2)}, u32[]{:S(2)}) %collective-permute-start.5) | collective-permute-done | bytes 16416 | tf_op jit(solution)/shard_map/while/body/eval_jaxpr/ppermute | solution.py:24
  372.8 6.1 collective-permute-start.8
  378.9 8.5 %collective-permute-start.4 = (bf16[16,512]{1,0:T(8,128)(2,1)S(1)}, bf16[16,512]{1,0:T(8,128)(2,1)S(1)}, u32[]{:S(2)}, u32[]{:S(2)}) collective-permute-start(bf16[16,512]{1,0:T(8,128)(2,1)S(1)} %copy.125), channel_id=1, source_target_pairs={{0,1},{1,2},{2,3},{3,4},{4,5},{5,6},{6,7},{7,8},{8,9},{9,10},{10,1... | collective-permute-start | bytes 49160 | tf_op jit(solution)/shard_map/while/body/eval_jaxpr/ppermute | solution.py:24
  390.6 8.4 %collective-permute-done.5 = bf16[16,512]{1,0:T(8,128)(2,1)S(1)} collective-permute-done((bf16[16,512]{1,0:T(8,128)(2,1)S(1)}, bf16[16,512]{1,0:T(8,128)(2,1)S(1)}, u32[]{:S(2)}, u32[]{:S(2)}) %collective-permute-start.5) | collective-permute-done | bytes 16416 | tf_op jit(solution)/shard_map/while/body/eval_jaxpr/ppermute | solution.py:24
  433.4 9.0 %collective-permute-start.4 = (bf16[16,512]{1,0:T(8,128)(2,1)S(1)}, bf16[16,512]{1,0:T(8,128)(2,1)S(1)}, u32[]{:S(2)}, u32[]{:S(2)}) collective-permute-start(bf16[16,512]{1,0:T(8,128)(2,1)S(1)} %copy.125), channel_id=1, source_target_pairs={{0,1},{1,2},{2,3},{3,4},{4,5},{5,6},{6,7},{7,8},{8,9},{9,10},{10,1... | collective-permute-start | bytes 49160 | tf_op jit(solution)/shard_map/while/body/eval_jaxpr/ppermute | solution.py:24
  445.1 9.0 %collective-permute-done.5 = bf16[16,512]{1,0:T(8,128)(2,1)S(1)} collective-permute-done((bf16[16,512]{1,0:T(8,128)(2,1)S(1)}, bf16[16,512]{1,0:T(8,128)(2,1)S(1)}, u32[]{:S(2)}, u32[]{:S(2)}) %collective-permute-start.5) | collective-permute-done | bytes 16416 | tf_op jit(solution)/shard_map/while/body/eval_jaxpr/ppermute | solution.py:24
  531.6 8.5 %collective-permute-start.8 = (f32[16,512]{1,0:T(8,128)S(1)}, f32[16,512]{1,0:T(8,128)S(1)}, u32[]{:S(2)}, u32[]{:S(2)}) collective-permute-start(f32[16,512]{1,0:T(8,128)S(1)} %add_add_fusion.4), channel_id=1, source_target_pairs={{0,1},{1,2},{2,3},{3,4},{4,5},{5,6},{6,7},{7,8},{8,9},{9,10},{10,1... | collective-permute-start | bytes 98312 | tf_op jit(solution)/shard_map/while/body/eval_jaxpr/ppermute | solution.py:24
  540.1 9.6 %collective-permute-start.4 = (bf16[16,512]{1,0:T(8,128)(2,1)S(1)}, bf16[16,512]{1,0:T(8,128)(2,1)S(1)}, u32[]{:S(2)}, u32[]{:S(2)}) collective-permute-start(bf16[16,512]{1,0:T(8,128)(2,1)S(1)} %copy.125), channel_id=1, source_target_pairs={{0,1},{1,2},{2,3},{3,4},{4,5},{5,6},{6,7},{7,8},{8,9},{9,10},{10,1... | collective-permute-start | bytes 49160 | tf_op jit(solution)/shard_map/while/body/eval_jaxpr/ppermute | solution.py:24
  551.8 9.5 %collective-permute-done.5 = bf16[16,512]{1,0:T(8,128)(2,1)S(1)} collective-permute-done((bf16[16,512]{1,0:T(8,128)(2,1)S(1)}, bf16[16,512]{1,0:T(8,128)(2,1)S(1)}, u32[]{:S(2)}, u32[]{:S(2)}) %collective-permute-start.5) | collective-permute-done | bytes 16416 | tf_op jit(solution)/shard_map/while/body/eval_jaxpr/ppermute | solution.py:24
  566.4 4.4 collective-permute-start.1
  597.0 9.8 %collective-permute-start.4 = (bf16[16,512]{1,0:T(8,128)(2,1)S(1)}, bf16[16,512]{1,0:T(8,128)(2,1)S(1)}, u32[]{:S(2)}, u32[]{:S(2)}) collective-permute-start(bf16[16,512]{1,0:T(8,128)(2,1)S(1)} %copy.125), channel_id=1, source_target_pairs={{0,1},{1,2},{2,3},{3,4},{4,5},{5,6},{6,7},{7,8},{8,9},{9,10},{10,1... | collective-permute-start | bytes 49160 | tf_op jit(solution)/shard_map/while/body/eval_jaxpr/ppermute | solution.py:24
  608.7 9.7 %collective-permute-done.5 = bf16[16,512]{1,0:T(8,128)(2,1)S(1)} collective-permute-done((bf16[16,512]{1,0:T(8,128)(2,1)S(1)}, bf16[16,512]{1,0:T(8,128)(2,1)S(1)}, u32[]{:S(2)}, u32[]{:S(2)}) %collective-permute-start.5) | collective-permute-done | bytes 16416 | tf_op jit(solution)/shard_map/while/body/eval_jaxpr/ppermute | solution.py:24
  651.9 9.8 %collective-permute-start.4 = (bf16[16,512]{1,0:T(8,128)(2,1)S(1)}, bf16[16,512]{1,0:T(8,128)(2,1)S(1)}, u32[]{:S(2)}, u32[]{:S(2)}) collective-permute-start(bf16[16,512]{1,0:T(8,128)(2,1)S(1)} %copy.125), channel_id=1, source_target_pairs={{0,1},{1,2},{2,3},{3,4},{4,5},{5,6},{6,7},{7,8},{8,9},{9,10},{10,1... | collective-permute-start | bytes 49160 | tf_op jit(solution)/shard_map/while/body/eval_jaxpr/ppermute | solution.py:24
  663.7 9.7 %collective-permute-done.5 = bf16[16,512]{1,0:T(8,128)(2,1)S(1)} collective-permute-done((bf16[16,512]{1,0:T(8,128)(2,1)S(1)}, bf16[16,512]{1,0:T(8,128)(2,1)S(1)}, u32[]{:S(2)}, u32[]{:S(2)}) %collective-permute-start.5) | collective-permute-done | bytes 16416 | tf_op jit(solution)/shard_map/while/body/eval_jaxpr/ppermute | solution.py:24
  (719 shorter events, 477.1 us)
Async XLA Ops:
  40.3 13.1 %collective-permute-start.7 = (f32[16,512]{1,0:T(8,128)S(1)}, f32[16,512]{1,0:T(8,128)S(1)}, u32[]{:S(2)}, u32[]{:S(2)}) collective-permute-start(f32[16,512]{1,0:T(8,128)S(1)} %slice_select_fusion.4), channel_id=1, source_target_pairs={{0,12},{12,0},{24,36},{36,24},{48,60},{60,48},{72,84},{84,72},{96,... | collective-permute-start | bytes 98312 | tf_op jit(solution)/shard_map/while/body/eval_jaxpr/ppermute | solution.py:18
  42.7 30.3 %collective-permute-start.11 = (f32[16,512]{1,0:T(8,128)S(1)}, f32[16,512]{1,0:T(8,128)S(1)}, u32[]{:S(2)}, u32[]{:S(2)}) collective-permute-start(f32[16,512]{1,0:T(8,128)S(1)} %add_add_fusion.5), channel_id=1, source_target_pairs={{0,1},{1,2},{2,3},{3,4},{4,5},{5,6},{6,7},{7,8},{8,9},{9,10},{10,1... | collective-permute-start | bytes 98312 | tf_op jit(solution)/shard_map/while/body/eval_jaxpr/ppermute | solution.py:24
  53.4 19.6 %collective-permute-start.8 = (f32[16,512]{1,0:T(8,128)S(1)}, f32[16,512]{1,0:T(8,128)S(1)}, u32[]{:S(2)}, u32[]{:S(2)}) collective-permute-start(f32[16,512]{1,0:T(8,128)S(1)} %add_add_fusion.4), channel_id=1, source_target_pairs={{0,1},{1,2},{2,3},{3,4},{4,5},{5,6},{6,7},{7,8},{8,9},{9,10},{10,1... | collective-permute-start | bytes 98312 | tf_op jit(solution)/shard_map/while/body/eval_jaxpr/ppermute | solution.py:24
  59.2 12.0 %collective-permute-start.4 = (bf16[16,512]{1,0:T(8,128)(2,1)S(1)}, bf16[16,512]{1,0:T(8,128)(2,1)S(1)}, u32[]{:S(2)}, u32[]{:S(2)}) collective-permute-start(bf16[16,512]{1,0:T(8,128)(2,1)S(1)} %copy.125), channel_id=1, source_target_pairs={{0,1},{1,2},{2,3},{3,4},{4,5},{5,6},{6,7},{7,8},{8,9},{9,10},{10,1... | collective-permute-start | bytes 49160 | tf_op jit(solution)/shard_map/while/body/eval_jaxpr/ppermute | solution.py:24
  61.2 11.8 %collective-permute-start.5 = (bf16[16,512]{1,0:T(8,128)(2,1)S(1)}, bf16[16,512]{1,0:T(8,128)(2,1)S(1)}, u32[]{:S(2)}, u32[]{:S(2)}) collective-permute-start(bf16[16,512]{1,0:T(8,128)(2,1)S(1)} %copy.126), channel_id=1, source_target_pairs={{0,1},{1,2},{2,3},{3,4},{4,5},{5,6},{6,7},{7,8},{8,9},{9,10},{10,1... | collective-permute-start | bytes 49160 | tf_op jit(solution)/shard_map/while/body/eval_jaxpr/ppermute | solution.py:24
  100.5 24.5 %collective-permute-start.11 = (f32[16,512]{1,0:T(8,128)S(1)}, f32[16,512]{1,0:T(8,128)S(1)}, u32[]{:S(2)}, u32[]{:S(2)}) collective-permute-start(f32[16,512]{1,0:T(8,128)S(1)} %add_add_fusion.5), channel_id=1, source_target_pairs={{0,1},{1,2},{2,3},{3,4},{4,5},{5,6},{6,7},{7,8},{8,9},{9,10},{10,1... | collective-permute-start | bytes 98312 | tf_op jit(solution)/shard_map/while/body/eval_jaxpr/ppermute | solution.py:24
  106.2 18.9 %collective-permute-start.8 = (f32[16,512]{1,0:T(8,128)S(1)}, f32[16,512]{1,0:T(8,128)S(1)}, u32[]{:S(2)}, u32[]{:S(2)}) collective-permute-start(f32[16,512]{1,0:T(8,128)S(1)} %add_add_fusion.4), channel_id=1, source_target_pairs={{0,1},{1,2},{2,3},{3,4},{4,5},{5,6},{6,7},{7,8},{8,9},{9,10},{10,1... | collective-permute-start | bytes 98312 | tf_op jit(solution)/shard_map/while/body/eval_jaxpr/ppermute | solution.py:24
  113.2 11.8 %collective-permute-start.5 = (bf16[16,512]{1,0:T(8,128)(2,1)S(1)}, bf16[16,512]{1,0:T(8,128)(2,1)S(1)}, u32[]{:S(2)}, u32[]{:S(2)}) collective-permute-start(bf16[16,512]{1,0:T(8,128)(2,1)S(1)} %copy.126), channel_id=1, source_target_pairs={{0,1},{1,2},{2,3},{3,4},{4,5},{5,6},{6,7},{7,8},{8,9},{9,10},{10,1... | collective-permute-start | bytes 49160 | tf_op jit(solution)/shard_map/while/body/eval_jaxpr/ppermute | solution.py:24
  152.9 28.9 %collective-permute-start.11 = (f32[16,512]{1,0:T(8,128)S(1)}, f32[16,512]{1,0:T(8,128)S(1)}, u32[]{:S(2)}, u32[]{:S(2)}) collective-permute-start(f32[16,512]{1,0:T(8,128)S(1)} %add_add_fusion.5), channel_id=1, source_target_pairs={{0,1},{1,2},{2,3},{3,4},{4,5},{5,6},{6,7},{7,8},{8,9},{9,10},{10,1... | collective-permute-start | bytes 98312 | tf_op jit(solution)/shard_map/while/body/eval_jaxpr/ppermute | solution.py:24
  154.9 26.9 %collective-permute-start.8 = (f32[16,512]{1,0:T(8,128)S(1)}, f32[16,512]{1,0:T(8,128)S(1)}, u32[]{:S(2)}, u32[]{:S(2)}) collective-permute-start(f32[16,512]{1,0:T(8,128)S(1)} %add_add_fusion.4), channel_id=1, source_target_pairs={{0,1},{1,2},{2,3},{3,4},{4,5},{5,6},{6,7},{7,8},{8,9},{9,10},{10,1... | collective-permute-start | bytes 98312 | tf_op jit(solution)/shard_map/while/body/eval_jaxpr/ppermute | solution.py:24
  163.5 11.8 %collective-permute-start.4 = (bf16[16,512]{1,0:T(8,128)(2,1)S(1)}, bf16[16,512]{1,0:T(8,128)(2,1)S(1)}, u32[]{:S(2)}, u32[]{:S(2)}) collective-permute-start(bf16[16,512]{1,0:T(8,128)(2,1)S(1)} %copy.125), channel_id=1, source_target_pairs={{0,1},{1,2},{2,3},{3,4},{4,5},{5,6},{6,7},{7,8},{8,9},{9,10},{10,1... | collective-permute-start | bytes 49160 | tf_op jit(solution)/shard_map/while/body/eval_jaxpr/ppermute | solution.py:24
  209.7 26.6 %collective-permute-start.11 = (f32[16,512]{1,0:T(8,128)S(1)}, f32[16,512]{1,0:T(8,128)S(1)}, u32[]{:S(2)}, u32[]{:S(2)}) collective-permute-start(f32[16,512]{1,0:T(8,128)S(1)} %add_add_fusion.5), channel_id=1, source_target_pairs={{0,1},{1,2},{2,3},{3,4},{4,5},{5,6},{6,7},{7,8},{8,9},{9,10},{10,1... | collective-permute-start | bytes 98312 | tf_op jit(solution)/shard_map/while/body/eval_jaxpr/ppermute | solution.py:24
  211.8 24.4 %collective-permute-start.8 = (f32[16,512]{1,0:T(8,128)S(1)}, f32[16,512]{1,0:T(8,128)S(1)}, u32[]{:S(2)}, u32[]{:S(2)}) collective-permute-start(f32[16,512]{1,0:T(8,128)S(1)} %add_add_fusion.4), channel_id=1, source_target_pairs={{0,1},{1,2},{2,3},{3,4},{4,5},{5,6},{6,7},{7,8},{8,9},{9,10},{10,1... | collective-permute-start | bytes 98312 | tf_op jit(solution)/shard_map/while/body/eval_jaxpr/ppermute | solution.py:24
  264.2 22.9 %collective-permute-start.11 = (f32[16,512]{1,0:T(8,128)S(1)}, f32[16,512]{1,0:T(8,128)S(1)}, u32[]{:S(2)}, u32[]{:S(2)}) collective-permute-start(f32[16,512]{1,0:T(8,128)S(1)} %add_add_fusion.5), channel_id=1, source_target_pairs={{0,1},{1,2},{2,3},{3,4},{4,5},{5,6},{6,7},{7,8},{8,9},{9,10},{10,1... | collective-permute-start | bytes 98312 | tf_op jit(solution)/shard_map/while/body/eval_jaxpr/ppermute | solution.py:24
  266.1 21.0 %collective-permute-start.8 = (f32[16,512]{1,0:T(8,128)S(1)}, f32[16,512]{1,0:T(8,128)S(1)}, u32[]{:S(2)}, u32[]{:S(2)}) collective-permute-start(f32[16,512]{1,0:T(8,128)S(1)} %add_add_fusion.4), channel_id=1, source_target_pairs={{0,1},{1,2},{2,3},{3,4},{4,5},{5,6},{6,7},{7,8},{8,9},{9,10},{10,1... | collective-permute-start | bytes 98312 | tf_op jit(solution)/shard_map/while/body/eval_jaxpr/ppermute | solution.py:24
  272.5 12.2 %collective-permute-start.4 = (bf16[16,512]{1,0:T(8,128)(2,1)S(1)}, bf16[16,512]{1,0:T(8,128)(2,1)S(1)}, u32[]{:S(2)}, u32[]{:S(2)}) collective-permute-start(bf16[16,512]{1,0:T(8,128)(2,1)S(1)} %copy.125), channel_id=1, source_target_pairs={{0,1},{1,2},{2,3},{3,4},{4,5},{5,6},{6,7},{7,8},{8,9},{9,10},{10,1... | collective-permute-start | bytes 49160 | tf_op jit(solution)/shard_map/while/body/eval_jaxpr/ppermute | solution.py:24
  314.9 27.4 %collective-permute-start.11 = (f32[16,512]{1,0:T(8,128)S(1)}, f32[16,512]{1,0:T(8,128)S(1)}, u32[]{:S(2)}, u32[]{:S(2)}) collective-permute-start(f32[16,512]{1,0:T(8,128)S(1)} %add_add_fusion.5), channel_id=1, source_target_pairs={{0,1},{1,2},{2,3},{3,4},{4,5},{5,6},{6,7},{7,8},{8,9},{9,10},{10,1... | collective-permute-start | bytes 98312 | tf_op jit(solution)/shard_map/while/body/eval_jaxpr/ppermute | solution.py:24
  317.9 24.5 %collective-permute-start.8 = (f32[16,512]{1,0:T(8,128)S(1)}, f32[16,512]{1,0:T(8,128)S(1)}, u32[]{:S(2)}, u32[]{:S(2)}) collective-permute-start(f32[16,512]{1,0:T(8,128)S(1)} %add_add_fusion.4), channel_id=1, source_target_pairs={{0,1},{1,2},{2,3},{3,4},{4,5},{5,6},{6,7},{7,8},{8,9},{9,10},{10,1... | collective-permute-start | bytes 98312 | tf_op jit(solution)/shard_map/while/body/eval_jaxpr/ppermute | solution.py:24
  323.0 12.2 %collective-permute-start.4 = (bf16[16,512]{1,0:T(8,128)(2,1)S(1)}, bf16[16,512]{1,0:T(8,128)(2,1)S(1)}, u32[]{:S(2)}, u32[]{:S(2)}) collective-permute-start(bf16[16,512]{1,0:T(8,128)(2,1)S(1)} %copy.125), channel_id=1, source_target_pairs={{0,1},{1,2},{2,3},{3,4},{4,5},{5,6},{6,7},{7,8},{8,9},{9,10},{10,1... | collective-permute-start | bytes 49160 | tf_op jit(solution)/shard_map/while/body/eval_jaxpr/ppermute | solution.py:24
  370.9 28.2 %collective-permute-start.11 = (f32[16,512]{1,0:T(8,128)S(1)}, f32[16,512]{1,0:T(8,128)S(1)}, u32[]{:S(2)}, u32[]{:S(2)}) collective-permute-start(f32[16,512]{1,0:T(8,128)S(1)} %add_add_fusion.5), channel_id=1, source_target_pairs={{0,1},{1,2},{2,3},{3,4},{4,5},{5,6},{6,7},{7,8},{8,9},{9,10},{10,1... | collective-permute-start | bytes 98312 | tf_op jit(solution)/shard_map/while/body/eval_jaxpr/ppermute | solution.py:24
  372.8 26.2 %collective-permute-start.8 = (f32[16,512]{1,0:T(8,128)S(1)}, f32[16,512]{1,0:T(8,128)S(1)}, u32[]{:S(2)}, u32[]{:S(2)}) collective-permute-start(f32[16,512]{1,0:T(8,128)S(1)} %add_add_fusion.4), channel_id=1, source_target_pairs={{0,1},{1,2},{2,3},{3,4},{4,5},{5,6},{6,7},{7,8},{8,9},{9,10},{10,1... | collective-permute-start | bytes 98312 | tf_op jit(solution)/shard_map/while/body/eval_jaxpr/ppermute | solution.py:24
  427.6 26.5 %collective-permute-start.11 = (f32[16,512]{1,0:T(8,128)S(1)}, f32[16,512]{1,0:T(8,128)S(1)}, u32[]{:S(2)}, u32[]{:S(2)}) collective-permute-start(f32[16,512]{1,0:T(8,128)S(1)} %add_add_fusion.5), channel_id=1, source_target_pairs={{0,1},{1,2},{2,3},{3,4},{4,5},{5,6},{6,7},{7,8},{8,9},{9,10},{10,1... | collective-permute-start | bytes 98312 | tf_op jit(solution)/shard_map/while/body/eval_jaxpr/ppermute | solution.py:24
  429.5 24.5 %collective-permute-start.8 = (f32[16,512]{1,0:T(8,128)S(1)}, f32[16,512]{1,0:T(8,128)S(1)}, u32[]{:S(2)}, u32[]{:S(2)}) collective-permute-start(f32[16,512]{1,0:T(8,128)S(1)} %add_add_fusion.4), channel_id=1, source_target_pairs={{0,1},{1,2},{2,3},{3,4},{4,5},{5,6},{6,7},{7,8},{8,9},{9,10},{10,1... | collective-permute-start | bytes 98312 | tf_op jit(solution)/shard_map/while/body/eval_jaxpr/ppermute | solution.py:24
  482.0 19.7 %collective-permute-start.11 = (f32[16,512]{1,0:T(8,128)S(1)}, f32[16,512]{1,0:T(8,128)S(1)}, u32[]{:S(2)}, u32[]{:S(2)}) collective-permute-start(f32[16,512]{1,0:T(8,128)S(1)} %add_add_fusion.5), channel_id=1, source_target_pairs={{0,1},{1,2},{2,3},{3,4},{4,5},{5,6},{6,7},{7,8},{8,9},{9,10},{10,1... | collective-permute-start | bytes 98312 | tf_op jit(solution)/shard_map/while/body/eval_jaxpr/ppermute | solution.py:24
  484.0 17.8 %collective-permute-start.8 = (f32[16,512]{1,0:T(8,128)S(1)}, f32[16,512]{1,0:T(8,128)S(1)}, u32[]{:S(2)}, u32[]{:S(2)}) collective-permute-start(f32[16,512]{1,0:T(8,128)S(1)} %add_add_fusion.4), channel_id=1, source_target_pairs={{0,1},{1,2},{2,3},{3,4},{4,5},{5,6},{6,7},{7,8},{8,9},{9,10},{10,1... | collective-permute-start | bytes 98312 | tf_op jit(solution)/shard_map/while/body/eval_jaxpr/ppermute | solution.py:24
  489.9 11.8 %collective-permute-start.5 = (bf16[16,512]{1,0:T(8,128)(2,1)S(1)}, bf16[16,512]{1,0:T(8,128)(2,1)S(1)}, u32[]{:S(2)}, u32[]{:S(2)}) collective-permute-start(bf16[16,512]{1,0:T(8,128)(2,1)S(1)} %copy.126), channel_id=1, source_target_pairs={{0,1},{1,2},{2,3},{3,4},{4,5},{5,6},{6,7},{7,8},{8,9},{9,10},{10,1... | collective-permute-start | bytes 49160 | tf_op jit(solution)/shard_map/while/body/eval_jaxpr/ppermute | solution.py:24
  529.6 31.8 %collective-permute-start.11 = (f32[16,512]{1,0:T(8,128)S(1)}, f32[16,512]{1,0:T(8,128)S(1)}, u32[]{:S(2)}, u32[]{:S(2)}) collective-permute-start(f32[16,512]{1,0:T(8,128)S(1)} %add_add_fusion.5), channel_id=1, source_target_pairs={{0,1},{1,2},{2,3},{3,4},{4,5},{5,6},{6,7},{7,8},{8,9},{9,10},{10,1... | collective-permute-start | bytes 98312 | tf_op jit(solution)/shard_map/while/body/eval_jaxpr/ppermute | solution.py:24
  531.6 29.8 %collective-permute-start.8 = (f32[16,512]{1,0:T(8,128)S(1)}, f32[16,512]{1,0:T(8,128)S(1)}, u32[]{:S(2)}, u32[]{:S(2)}) collective-permute-start(f32[16,512]{1,0:T(8,128)S(1)} %add_add_fusion.4), channel_id=1, source_target_pairs={{0,1},{1,2},{2,3},{3,4},{4,5},{5,6},{6,7},{7,8},{8,9},{9,10},{10,1... | collective-permute-start | bytes 98312 | tf_op jit(solution)/shard_map/while/body/eval_jaxpr/ppermute | solution.py:24
  591.0 27.4 %collective-permute-start.11 = (f32[16,512]{1,0:T(8,128)S(1)}, f32[16,512]{1,0:T(8,128)S(1)}, u32[]{:S(2)}, u32[]{:S(2)}) collective-permute-start(f32[16,512]{1,0:T(8,128)S(1)} %add_add_fusion.5), channel_id=1, source_target_pairs={{0,1},{1,2},{2,3},{3,4},{4,5},{5,6},{6,7},{7,8},{8,9},{9,10},{10,1... | collective-permute-start | bytes 98312 | tf_op jit(solution)/shard_map/while/body/eval_jaxpr/ppermute | solution.py:24
  593.0 25.5 %collective-permute-start.8 = (f32[16,512]{1,0:T(8,128)S(1)}, f32[16,512]{1,0:T(8,128)S(1)}, u32[]{:S(2)}, u32[]{:S(2)}) collective-permute-start(f32[16,512]{1,0:T(8,128)S(1)} %add_add_fusion.4), channel_id=1, source_target_pairs={{0,1},{1,2},{2,3},{3,4},{4,5},{5,6},{6,7},{7,8},{8,9},{9,10},{10,1... | collective-permute-start | bytes 98312 | tf_op jit(solution)/shard_map/while/body/eval_jaxpr/ppermute | solution.py:24
  647.2 26.2 %collective-permute-start.11 = (f32[16,512]{1,0:T(8,128)S(1)}, f32[16,512]{1,0:T(8,128)S(1)}, u32[]{:S(2)}, u32[]{:S(2)}) collective-permute-start(f32[16,512]{1,0:T(8,128)S(1)} %add_add_fusion.5), channel_id=1, source_target_pairs={{0,1},{1,2},{2,3},{3,4},{4,5},{5,6},{6,7},{7,8},{8,9},{9,10},{10,1... | collective-permute-start | bytes 98312 | tf_op jit(solution)/shard_map/while/body/eval_jaxpr/ppermute | solution.py:24
  649.2 24.2 %collective-permute-start.8 = (f32[16,512]{1,0:T(8,128)S(1)}, f32[16,512]{1,0:T(8,128)S(1)}, u32[]{:S(2)}, u32[]{:S(2)}) collective-permute-start(f32[16,512]{1,0:T(8,128)S(1)} %add_add_fusion.4), channel_id=1, source_target_pairs={{0,1},{1,2},{2,3},{3,4},{4,5},{5,6},{6,7},{7,8},{8,9},{9,10},{10,1... | collective-permute-start | bytes 98312 | tf_op jit(solution)/shard_map/while/body/eval_jaxpr/ppermute | solution.py:24
  (119 other events, 745.5 us)
where the time goes:
time: 683 us; the launch traced here: 679 us
  starting transfers between devices  462 us (68%)
  waiting for transfers between devices  144 us (21%)
  matrix products  24.3 us (4%)
  other arithmetic  19.5 us (3%)
  local copies, waits for them, and re-layouts  14.2 us (2%)
  loops' own time  12.9 us (2%)
    ppermute x96, starting transfers between devices, from_partner(): lax.ppermute(array, axis, [(i, i ^ 1 << bit) for i in range(lax.axis_size...  245 us
    ppermute x48, starting transfers between devices, shifted(): return lax.ppermute(value, axis, pairs)  218 us
    ppermute x48, waiting for transfers between devices, shifted(): return lax.ppermute(value, axis, pairs)  102 us
    ppermute x96, waiting for transfers between devices, from_partner(): lax.ppermute(array, axis, [(i, i ^ 1 << bit) for i in range(lax.axis_size...  42.4 us
  transfers between devices with their start and end apart: 144, of which 47 were waited for; matrix products, arithmetic and copies ran while one was open for 0% of the time, Pallas kernels for 0%

commit v1 on v0

v1 whole, which is shorter than its diff:
```python
import jax
import jax.numpy as jnp
from jax import lax
from jax.experimental import pallas as pl
from jax.experimental.pallas import tpu as pltpu
from jax.sharding import PartitionSpec as P

HQ = 20
HK = 4
DH = 128
R = HQ // HK
RT = 128
PB = 16
W = HK * DH
NX = 4
NZ = 6
CT = NZ * 2 * PB
SCALE = 1.0 / DH**0.5
LOG2E = 1.4426950408889634
f32, bf16 = jnp.float32, jnp.bfloat16
NT = (((1,), (1,)), ((), ()))
NN = (((1,), (0,)), ((), ()))
MESH = pl.DeviceIdType.MESH

Z0, ZD, ZR, XP, XM, XR, CG = 0, 1, 3, 5, 11, 17, 23
RC, RA, RB, RZ0, RZ1, RD = 27, 31, 33, 37, 38, 39
NSEM = 41


def dot(a, b, dims):
    return lax.dot_general(a, b, dims, preferred_element_type=f32)


def kernel(
    meta, q_hbm, kr_hbm, vr_hbm, do_hbm, fo_hbm, lse_hbm, pk_hbm, pv_hbm,
    gq_hbm, gkr_hbm, gvr_hbm, gpk_hbm, gpv_hbm,
    q_v, do_v, fo_v, lse_v, kr_v, vr_v, gq_v, gkr_v, gvr_v, gp_v,
    qs, dos, col, rows, gacc,
    buf, part, rc, summed, ra, rb, zsend, rz, rd, agg, own,
    lsem, osem, send, recv,
):
    dp, rs = lax.axis_index("dp"), lax.axis_index("resp")
    base = dp // 4 * 4
    zl, c = dp % 4 // 2, dp % 2
    x, zh = rs // 3, rs % 3
    dn = 2 * zl - 1
    up_zh, down_zh = (zh + 1) % 3, (zh + 2) % 3
    near_zh, far_zh = (zh + dn + 3) % 3, (zh - dn + 3) % 3
    z = zh * 2 + zl
    length, seen = meta[0], meta[1]

    def dev(xx, hh, ll, cc):
        return (base + ll * 2 + cc, xx * 3 + hh)

    right, left = (x + 1) % 4, (x + 3) % 4
    sibling = dev(x, zh, zl, 1 - c)
    partner = dev(x, zh, 1 - zl, c)
    xr, xl = dev(right, zh, zl, c), dev(left, zh, zl, c)
    up, down = dev(x, up_zh, 0, c), dev(x, down_zh, 1, c)
    near = [dev(x, near_zh, i, c) for i in range(2)]

    loads = [
        pltpu.make_async_copy(pk_hbm, buf.at[x, z, c, :, 0:W], lsem.at[0]),
        pltpu.make_async_copy(pv_hbm, buf.at[x, z, c, :, W : 2 * W], lsem.at[1]),
        pltpu.make_async_copy(do_hbm, do_v, lsem.at[2]),
        pltpu.make_async_copy(fo_hbm, fo_v, lsem.at[3]),
        pltpu.make_async_copy(lse_hbm, lse_v, lsem.at[4]),
        pltpu.make_async_copy(q_hbm, q_v, lsem.at[5]),
        pltpu.make_async_copy(kr_hbm, kr_v, lsem.at[6]),
        pltpu.make_async_copy(vr_hbm, vr_v, lsem.at[7]),
    ]
    for copy in loads:
        copy.start()

    barrier = pltpu.get_barrier_semaphore()
    for other in (sibling, partner, xr, xl, near[0], near[1], up, down):
        pl.semaphore_signal(barrier, inc=1, device_id=other, device_id_type=MESH)

    sends = []

    def push(src, dst, index, device):
        copy = pltpu.make_async_remote_copy(
            src_ref=src, dst_ref=dst, send_sem=send.at[len(sends)], recv_sem=recv.at[index],
            device_id=device, device_id_type=MESH,
        )
        copy.start()
        sends.append(copy)

    def arrived(ref, index):
        pltpu.make_async_copy(ref, ref, recv.at[index]).wait()

    for copy in loads[2:5]:
        copy.wait()
    live = lax.broadcasted_iota(jnp.int32, (RT, 1), 0) < length
    col[0, :, 0:HQ] = jnp.where(live, lse_v[...] * LOG2E, 1e30)
    for h in range(HQ):
        sl = slice(h * DH, (h + 1) * DH)
        col[1, :, h : h + 1] = jnp.sum(
            do_v[:, sl].astype(f32) * fo_v[:, sl].astype(f32), axis=1, keepdims=True
        )
    rows[0] = col[0].T
    rows[1] = col[1].T
    loads[5].wait()
    for g in range(HK):
        for r in range(R):
            sl = slice((g * R + r) * DH, (g * R + r + 1) * DH)
            qs[g, r * RT : (r + 1) * RT, :] = q_v[:, sl]
            dos[g, r * RT : (r + 1) * RT, :] = do_v[:, sl]

    loads[0].wait()
    loads[1].wait()
    pl.semaphore_wait(barrier, 8)

    slot_z = [z, zh * 2 + 1 - zl, near_zh * 2, near_zh * 2 + 1, far_zh * 2, far_zh * 2 + 1]

    def block(xx, s):
        return buf.at[xx, slot_z[s], c]

    def spread(s):
        push(block(x, s), block(x, s), XP + s, xr)
        push(block(x, s), block(x, s), XM + s, xl)

    push(block(x, 0), block(x, 0), ZD + zl, up)
    push(block(x, 0), block(x, 0), ZD + zl, down)
    push(block(x, 0), block(x, 0), Z0, partner)
    spread(0)

    def pair(k, v, g, mask):
        qh, dh = qs[g], dos[g]
        lse = jnp.concatenate([rows[0, g * R + r : g * R + r + 1, :] for r in range(R)], axis=1)
        dlt = jnp.concatenate([rows[1, g * R + r : g * R + r + 1, :] for r in range(R)], axis=1)
        p = jnp.exp2(dot(k, qh, NT) * (SCALE * LOG2E) - lse)
        if mask is not None:
            p = jnp.where(mask, p, 0.0)
        ds = (p * (dot(v, dh, NT) - dlt)).astype(bf16)
        gv = dot(p.astype(bf16), dh, NN)
        gk = dot(ds, qh, NN) * SCALE
        return dot(k.T, ds, NN), gk, gv

    loads[6].wait()
    loads[7].wait()
    token = lax.broadcasted_iota(jnp.int32, (RT, R * RT), 0)
    query = lax.broadcasted_iota(jnp.int32, (RT, R * RT), 1) % RT
    for g in range(HK):
        ls = slice(g * DH, (g + 1) * DH)
        gq, gk, gv = pair(kr_v[:, ls], vr_v[:, ls], g, token <= query)
        gkr_v[:, ls] = gk.astype(bf16)
        gvr_v[:, ls] = gv.astype(bf16)
        gacc[g] = gq
    outs = [
        pltpu.make_async_copy(gkr_v, gkr_hbm, osem.at[0]),
        pltpu.make_async_copy(gvr_v, gvr_hbm, osem.at[1]),
    ]
    for copy in outs:
        copy.start()

    arrived(block(x, 1), Z0)
    spread(1)
    for i in range(2):
        arrived(block(x, 2 + i), ZD + i)
        push(block(x, 2 + i), block(x, 2 + i), ZR + i, partner)
        spread(2 + i)
    for i in range(2):
        arrived(block(x, 4 + i), ZR + i)
        spread(4 + i)
    push(buf.at[x, :, c], buf.at[x, :, c], CG, sibling)

    for s in range(NZ):
        arrived(block(left, s), XP + s)
        if s % 2 == 0:
            push(block(left, s), block(left, s), XR + s, xr)
        arrived(block(right, s), XM + s)
        if s % 2 == 1:
            push(block(right, s), block(right, s), XR + s, xl)
    push(buf.at[right, :, c], buf.at[right, :, c], CG + 1, sibling)
    push(buf.at[left, :, c], buf.at[left, :, c], CG + 3, sibling)

    def work(d):
        xx = (x + d) % 4
        arrived(buf.at[xx, :, 1 - c], CG + [0, 1, 2, 3][d])
        seen_here = lax.broadcasted_iota(jnp.int32, (CT, 1), 0) + xx * CT < seen * PB
        none = jnp.zeros((), bf16)
        for g in range(HK):
            ks = slice(g * DH, (g + 1) * DH)
            vs = slice(W + g * DH, W + (g + 1) * DH)
            k = jnp.where(seen_here, buf[xx, :, :, :, ks].reshape(CT, DH), none)
            v = jnp.where(seen_here, buf[xx, :, :, :, vs].reshape(CT, DH), none)
            gq, gk, gv = pair(k, v, g, None)
            gacc[g] += gq
            gk = jnp.where(seen_here, gk, 0.0).astype(bf16)
            gv = jnp.where(seen_here, gv, 0.0).astype(bf16)
            part[xx, :, :, :, ks] = gk.reshape(NZ, 2, PB, DH)
            part[xx, :, :, :, vs] = gv.reshape(NZ, 2, PB, DH)
        push(part.at[xx, :, 1 - c], rc.at[d], RC + d, sibling)

    def core_sum(d, lo, hi):
        xx = (x + d) % 4
        total = part[xx, lo:hi, c].astype(f32) + rc[d, lo:hi].astype(f32)
        return total

    work(0)
    for s in range(NZ):
        arrived(block((x + 2) % 4, s), XR + s)
    push(buf.at[(x + 2) % 4, :, c], buf.at[(x + 2) % 4, :, c], CG + 2, sibling)
    work(1)
    work(2)
    arrived(rc.at[2], RC + 2)
    summed[2] = core_sum(2, 0, NZ).astype(bf16)
    push(summed.at[2, 0:3], ra.at[0], RA, xr)
    push(summed.at[2, 3:6], ra.at[1], RA + 1, xl)
    arrived(rc.at[1], RC + 1)
    summed[1, 3:6] = core_sum(1, 3, 6).astype(bf16)
    push(summed.at[1, 3:6], rb.at[0, 3:6], RB + 1, xr)
    work(3)
    for g in range(HK):
        for r in range(R):
            sl = slice((g * R + r) * DH, (g * R + r + 1) * DH)
            gq_v[:, sl] = (gacc[g, :, r * RT : (r + 1) * RT].T * SCALE).astype(bf16)
    outs.append(pltpu.make_async_copy(gq_v, gq_hbm, osem.at[2]))
    outs[-1].start()
    arrived(rc.at[3], RC + 3)
    summed[3, 0:3] = core_sum(3, 0, 3).astype(bf16)
    push(summed.at[3, 0:3], rb.at[1, 0:3], RB + 2, xl)
    arrived(ra.at[0], RA)
    summed[1, 0:3] = (core_sum(1, 0, 3) + ra[0].astype(f32)).astype(bf16)
    push(summed.at[1, 0:3], rb.at[0, 0:3], RB, xr)
    arrived(ra.at[1], RA + 1)
    summed[3, 3:6] = (core_sum(3, 3, 6) + ra[1].astype(f32)).astype(bf16)
    push(summed.at[3, 3:6], rb.at[1, 3:6], RB + 3, xl)

    arrived(rc.at[0], RC)
    arrived(rb.at[0, 3:6], RB + 1)
    arrived(rb.at[1, 0:3], RB + 2)
    arrived(rb.at[0, 0:3], RB)
    arrived(rb.at[1, 3:6], RB + 3)

    def x_sum(first, count):
        at = pl.ds(first, count)
        return (
            part[x, at, c].astype(f32) + rc[0, at].astype(f32)
        ) + (rb[0, at].astype(f32) + rb[1, at].astype(f32))

    zsend[0:2] = x_sum(far_zh * 2, 2).astype(bf16)
    push(zsend.at[0:2], rz.at[0:2], RZ0, partner)
    zsend[2:3] = x_sum(zh * 2 + 1 - zl, 1).astype(bf16)
    push(zsend.at[2], rz.at[2], RZ1, partner)
    own[...] = x_sum(z, 1)[0]
    agg_own = x_sum(near_zh * 2, 2)
    arrived(rz.at[0:2], RZ0)
    agg[...] = (agg_own + rz[0:2].astype(f32)).astype(bf16)
    for i in range(2):
        push(agg.at[i], rd.at[zl], RD + zl, near[i])
    arrived(rz.at[2], RZ1)
    arrived(rd.at[0], RD)
    arrived(rd.at[1], RD + 1)
    total = (own[...] + rz[2].astype(f32)) + (rd[0].astype(f32) + rd[1].astype(f32))
    gp_v[...] = total
    outs.append(pltpu.make_async_copy(gp_v.at[:, 0:W], gpk_hbm, osem.at[3]))
    outs.append(pltpu.make_async_copy(gp_v.at[:, W : 2 * W], gpv_hbm, osem.at[4]))
    outs[-2].start()
    outs[-1].start()
    for copy in sends:
        copy.wait_send()
    for copy in outs:
        copy.wait()


NSEND = 41


def shards(queries, resp_keys, resp_values, grad_out, forward_out, log_norm, prompt_keys, prompt_values, resp_len, seen_blocks):
    meta = jnp.concatenate([resp_len, seen_blocks])
    shape = jax.ShapeDtypeStruct
    any_space = pl.BlockSpec(memory_space=pl.ANY)
    vmem = pltpu.VMEM
    gq, gkr, gvr, gpk, gpv = pl.pallas_call(
        kernel,
        in_specs=[pl.BlockSpec(memory_space=pltpu.SMEM)] + [any_space] * 8,
        out_specs=[any_space] * 5,
        out_shape=[
            shape((RT, HQ * DH), bf16),
            shape((RT, W), bf16),
            shape((RT, W), bf16),
            shape((PB, W), f32),
            shape((PB, W), f32),
        ],
        scratch_shapes=[
            vmem((RT, HQ * DH), bf16),
            vmem((RT, HQ * DH), bf16),
            vmem((RT, HQ * DH), bf16),
            vmem((RT, HQ), f32),
            vmem((RT, W), bf16),
            vmem((RT, W), bf16),
            vmem((RT, HQ * DH), bf16),
            vmem((RT, W), bf16),
            vmem((RT, W), bf16),
            vmem((PB, 2 * W), f32),
            vmem((HK, R * RT, DH), bf16),
            vmem((HK, R * RT, DH), bf16),
            vmem((2, RT, DH), f32),
            vmem((2, DH, RT), f32),
            vmem((HK, DH, R * RT), f32),
            vmem((NX, NZ, 2, PB, 2 * W), bf16),
            vmem((NX, NZ, 2, PB, 2 * W), bf16),
            vmem((NX, NZ, PB, 2 * W), bf16),
            vmem((NX, NZ, PB, 2 * W), bf16),
            vmem((2, 3, PB, 2 * W), bf16),
            vmem((2, NZ, PB, 2 * W), bf16),
            vmem((3, PB, 2 * W), bf16),
            vmem((3, PB, 2 * W), bf16),
            vmem((2, PB, 2 * W), bf16),
            vmem((2, PB, 2 * W), bf16),
            vmem((PB, 2 * W), f32),
            pltpu.SemaphoreType.DMA((8,)),
            pltpu.SemaphoreType.DMA((5,)),
            pltpu.SemaphoreType.DMA((NSEND,)),
            pltpu.SemaphoreType.DMA((NSEM,)),
        ],
        compiler_params=pltpu.CompilerParams(collective_id=0, has_side_effects=True),
        name="attention_backward",
    )(meta, queries[0], resp_keys[0], resp_values[0], grad_out[0], forward_out[0], log_norm[0], prompt_keys[0], prompt_values[0])
    return gq[None], gkr[None], gvr[None], gpk[None], gpv[None]


def solution(mesh):
    rows = P(("dp", "resp"), None, None)
    prompt = P("resp", "dp", None)
    one = P(("dp", "resp"))
    return jax.shard_map(
        shards,
        mesh=mesh,
        in_specs=(rows,) * 6 + (prompt,) * 2 + (one,) * 2,
        out_specs=(rows,) * 3 + (prompt,) * 2,
        check_vma=False,
    )
```

time: 683 us -> 62.8 us (0.09)
  the two profiles are of different devices: /device:TPU:144 before, /device:TPU:32 now
where the time goes in v1:
time: 62.8 us; the launch traced here: 62.4 us
  Pallas kernels  54 us (86%)
  local copies, waits for them, and re-layouts  5.84 us (9%)
  between operations  1.97 us (3%)
    pallas_call x1, Pallas kernels, shards(): pl.pallas_call(kernel, in_specs=[pl.BlockSpec(memory_space=pltpu.SMEM)] +...  54 us
    unnamed x16, local copies, waits for them, and re-layouts  5.84 us

profile of v1, /device:TPU:32, one launch (start us, length us, event | category | flops | bytes accessed | tf_op | source)
XLA Modules:
  0.0 62.4 jit_solution(16414746061777676056)
XLA Ops:
  0.6 0.0 copy-start.4
  1.9 0.6 pad_add_fusion.meta
  2.5 0.0 copy-done.4
  2.5 0.7 %copy.15 = f32[1,128,20]{2,1,0:T(8,128)} copy(f32[1,128,20]{1,0,2:T(1,128)S(1)} %copy-done.4) | data formatting | bytes 20480 | tf_op args[5]
  3.3 54.0 %attention_backward.1 = (bf16[128,2560]{1,0:T(8,128)(2,1)}, bf16[128,512]{1,0:T(8,128)(2,1)}, bf16[128,512]{1,0:T(8,128)(2,1)}, f32[16,512]{1,0:T(8,128)}, f32[16,512]{1,0:T(8,128)}) custom-call(s32[2]{0:T(128)} %pad_add_fusion.meta, bf16[128,2560]{1,0:T(8,128)(2,1)} %bitcast.13, bf16[128,512]{1,0:T(8,128)(2,1)} %bitcast.18, bf16[128,512]{1,0:T(8,128)(2,1)} %bitcast.19, ...), custom_call_target="tpu_custom_call" | custom-call | tf_op jit(solution)/shard_map/attention_backward/pallas_call | solution.py:276
  57.3 0.0 copy-start.1
  57.3 2.0 %copy.23 = bf16[1,128,2560]{2,1,0:T(8,128)(2,1)} copy(bf16[1,128,2560]{2,1,0:T(8,128)(2,1)} %bitcast.16) | data formatting | bytes 1310720
  59.3 0.0 copy-done.1
  59.3 0.0 copy-start
  59.3 0.7 %copy.24 = bf16[1,128,512]{2,1,0:T(8,128)(2,1)} copy(bf16[1,128,512]{2,1,0:T(8,128)(2,1)S(1)} %bitcast.21) | data formatting | bytes 262144
  59.9 0.3 copy-done
  60.2 0.0 copy-start.3
  60.2 0.7 %copy.25 = bf16[1,128,512]{2,1,0:T(8,128)(2,1)} copy(bf16[1,128,512]{2,1,0:T(8,128)(2,1)S(1)} %bitcast.20) | data formatting | bytes 262144
  60.9 0.1 copy-done.3
  61.0 0.0 copy-start.2
  61.0 0.6 copy.26
  61.6 0.2 copy-done.2
  61.8 0.6 copy.27
Async XLA Ops:
  0.6 1.9 %copy-start.4 = (f32[1,128,20]{1,0,2:T(1,128)S(1)}, f32[1,128,20]{1,0,2:T(1,128)}, u32[]{:S(2)}) copy-start(f32[1,128,20]{1,0,2:T(1,128)} %param.15) | copy-start | bytes 30724
  57.3 2.0 %copy-start.1 = (bf16[128,512]{1,0:T(8,128)(2,1)S(1)}, bf16[128,512]{1,0:T(8,128)(2,1)}, u32[]{:S(2)}) copy-start(bf16[128,512]{1,0:T(8,128)(2,1)} %get-tuple-element.11) | copy-start | bytes 393220
  59.3 1.0 %copy-start = (bf16[128,512]{1,0:T(8,128)(2,1)S(1)}, bf16[128,512]{1,0:T(8,128)(2,1)}, u32[]{:S(2)}) copy-start(bf16[128,512]{1,0:T(8,128)(2,1)} %get-tuple-element.12) | copy-start | bytes 393220
  60.2 0.8 %copy-start.3 = (f32[16,512]{1,0:T(8,128)S(1)}, f32[16,512]{1,0:T(8,128)}, u32[]{:S(2)}) copy-start(f32[16,512]{1,0:T(8,128)} %get-tuple-element.13) | copy-start | bytes 98308
  61.0 0.8 %copy-start.2 = (f32[16,512]{1,0:T(8,128)S(1)}, f32[16,512]{1,0:T(8,128)}, u32[]{:S(2)}) copy-start(f32[16,512]{1,0:T(8,128)} %get-tuple-element.14) | copy-start | bytes 98308

commit v2 on v1

v2 whole, which is shorter than its diff:
```python
import jax
import jax.numpy as jnp
from jax import lax
from jax.experimental import pallas as pl
from jax.experimental.pallas import tpu as pltpu
from jax.sharding import PartitionSpec as P

HQ = 20
HK = 4
DH = 128
R = HQ // HK
RT = 128
PB = 16
W = HK * DH
NX = 4
NZ = 6
CT = NZ * 2 * PB
SCALE = 1.0 / DH**0.5
LOG2E = 1.4426950408889634
f32, bf16 = jnp.float32, jnp.bfloat16
NT = (((1,), (1,)), ((), ()))
NN = (((1,), (0,)), ((), ()))
MESH = pl.DeviceIdType.MESH

Z0, ZD, ZR, XP, XM, XR, CG = 0, 1, 3, 5, 11, 17, 23
RC, RA, RB, RZ0, RZ1, RD = 27, 35, 39, 47, 49, 51
NSEM = 55


def dot(a, b, dims):
    return lax.dot_general(a, b, dims, preferred_element_type=f32)


def kernel(
    len_hbm, seen_hbm, q_hbm, kr_hbm, vr_hbm, do_hbm, fo_hbm, lse_hbm, pk_hbm, pv_hbm,
    gq_hbm, gkr_hbm, gvr_hbm, gpk_hbm, gpv_hbm,
    q_v, do_v, fo_v, lse_v, kr_v, vr_v, gq_v, gkr_v, gvr_v, gp_v,
    meta, qs, dos, col, rows, gacc,
    buf, part, rc, summed, ra, rb, zsend, rz, rd, agg, own_near,
    lsem, osem, send, recv,
):
    dp, rs = lax.axis_index("dp"), lax.axis_index("resp")
    base = dp // 4 * 4
    zl, c = dp % 4 // 2, dp % 2
    x, zh = rs // 3, rs % 3
    dn = 2 * zl - 1
    up_zh, down_zh = (zh + 1) % 3, (zh + 2) % 3
    near_zh, far_zh = (zh + dn + 3) % 3, (zh - dn + 3) % 3
    z = zh * 2 + zl

    def dev(xx, hh, ll, cc):
        return (base + ll * 2 + cc, xx * 3 + hh)

    right, left, over = (x + 1) % 4, (x + 3) % 4, (x + 2) % 4
    sibling = dev(x, zh, zl, 1 - c)
    partner = dev(x, zh, 1 - zl, c)
    xr, xl = dev(right, zh, zl, c), dev(left, zh, zl, c)
    up, down = dev(x, up_zh, 0, c), dev(x, down_zh, 1, c)
    near = [dev(x, near_zh, i, c) for i in range(2)]

    loads = [
        pltpu.make_async_copy(pk_hbm, buf.at[x, z, c, :, 0:W], lsem.at[0]),
        pltpu.make_async_copy(pv_hbm, buf.at[x, z, c, :, W : 2 * W], lsem.at[1]),
        pltpu.make_async_copy(do_hbm, do_v, lsem.at[2]),
        pltpu.make_async_copy(fo_hbm, fo_v, lsem.at[3]),
        pltpu.make_async_copy(lse_hbm, lse_v, lsem.at[4]),
        pltpu.make_async_copy(q_hbm, q_v, lsem.at[5]),
        pltpu.make_async_copy(kr_hbm, kr_v, lsem.at[6]),
        pltpu.make_async_copy(vr_hbm, vr_v, lsem.at[7]),
        pltpu.make_async_copy(len_hbm, meta.at[0], lsem.at[8]),
        pltpu.make_async_copy(seen_hbm, meta.at[1], lsem.at[9]),
    ]
    for copy in loads[:2]:
        copy.start()

    barrier = pltpu.get_barrier_semaphore()
    for other in (sibling, partner, xr, xl, near[0], near[1], up, down):
        pl.semaphore_signal(barrier, inc=1, device_id=other, device_id_type=MESH)
    for copy in loads[2:]:
        copy.start()

    sends = []

    def push(src, dst, index, device):
        copy = pltpu.make_async_remote_copy(
            src_ref=src, dst_ref=dst, send_sem=send.at[len(sends)], recv_sem=recv.at[index],
            device_id=device, device_id_type=MESH,
        )
        copy.start()
        sends.append(copy)

    def arrived(ref, index):
        pltpu.make_async_copy(ref, ref, recv.at[index]).wait()

    loads[0].wait()
    loads[1].wait()
    pl.semaphore_wait(barrier, 8)

    slot_z = [z, zh * 2 + 1 - zl, near_zh * 2, near_zh * 2 + 1, far_zh * 2, far_zh * 2 + 1]

    def block(xx, s):
        return buf.at[xx, slot_z[s], c]

    def twin(dx, xx, s):
        push(block(xx, s), block(xx, s), CG + dx, sibling)

    def spread(s):
        push(block(x, s), block(x, s), XP + s, xr)
        push(block(x, s), block(x, s), XM + s, xl)
        twin(0, x, s)

    push(block(x, 0), block(x, 0), ZD + zl, up)
    push(block(x, 0), block(x, 0), ZD + zl, down)
    push(block(x, 0), block(x, 0), Z0, partner)
    spread(0)

    for copy in loads[2:5] + loads[8:]:
        copy.wait()
    length, seen = meta[0, 0], meta[1, 0]
    live = lax.broadcasted_iota(jnp.int32, (1, RT), 1) < length
    for h in range(HQ):
        sl = slice(h * DH, (h + 1) * DH)
        rows[0, h : h + 1, :] = jnp.where(live, lse_v[h] * LOG2E, 1e30)
        col[:, h : h + 1] = jnp.sum(
            do_v[:, sl].astype(f32) * fo_v[:, sl].astype(f32), axis=1, keepdims=True
        )
    rows[1] = col[...].T
    loads[5].wait()
    for g in range(HK):
        for r in range(R):
            sl = slice((g * R + r) * DH, (g * R + r + 1) * DH)
            qs[g, r * RT : (r + 1) * RT, :] = q_v[:, sl]
            dos[g, r * RT : (r + 1) * RT, :] = do_v[:, sl]

    def pair(k, v, g, mask):
        qh, dh = qs[g], dos[g]
        lse = jnp.concatenate([rows[0, g * R + r : g * R + r + 1, :] for r in range(R)], axis=1)
        dlt = jnp.concatenate([rows[1, g * R + r : g * R + r + 1, :] for r in range(R)], axis=1)
        p = jnp.exp2(dot(k, qh, NT) * (SCALE * LOG2E) - lse)
        if mask is not None:
            p = jnp.where(mask, p, 0.0)
        ds = (p * (dot(v, dh, NT) - dlt)).astype(bf16)
        gv = dot(p.astype(bf16), dh, NN)
        gk = dot(ds, qh, NN) * SCALE
        return dot(k.T, ds, NN), gk, gv

    token = lax.broadcasted_iota(jnp.int32, (RT, R * RT), 0)
    query = lax.broadcasted_iota(jnp.int32, (RT, R * RT), 1) % RT

    def own_tokens(g):
        ls = slice(g * DH, (g + 1) * DH)
        gq, gk, gv = pair(kr_v[:, ls], vr_v[:, ls], g, token <= query)
        gkr_v[:, ls] = gk.astype(bf16)
        gvr_v[:, ls] = gv.astype(bf16)
        gacc[g] = gq

    def hand_on(s):
        arrived(block(left, s), XP + s)
        if s % 2 == 0:
            push(block(left, s), block(left, s), XR + s, xr)
        arrived(block(right, s), XM + s)
        if s % 2 == 1:
            push(block(right, s), block(right, s), XR + s, xl)
        twin(3, left, s)
        twin(1, right, s)

    def last_of(s):
        arrived(block(over, s), XR + s)
        twin(2, over, s)

    def work(d, half):
        xx = (x + d) % 4
        if half == 0:
            arrived(buf.at[xx, :, 1 - c], CG + d)
        seen_here = lax.broadcasted_iota(jnp.int32, (CT, 1), 0) + xx * CT < seen * PB
        none = jnp.zeros((), bf16)
        for g in (2 * half, 2 * half + 1):
            ks = slice(g * DH, (g + 1) * DH)
            vs = slice(W + g * DH, W + (g + 1) * DH)
            k = jnp.where(seen_here, buf[xx, :, :, :, ks].reshape(CT, DH), none)
            v = jnp.where(seen_here, buf[xx, :, :, :, vs].reshape(CT, DH), none)
            gq, gk, gv = pair(k, v, g, None)
            gacc[g] += gq
            gk = jnp.where(seen_here, gk, 0.0).astype(bf16)
            gv = jnp.where(seen_here, gv, 0.0).astype(bf16)
            at = 2 * g * DH
            part[xx, :, :, :, at : at + DH] = gk.reshape(NZ, 2, PB, DH)
            part[xx, :, :, :, at + DH : at + 2 * DH] = gv.reshape(NZ, 2, PB, DH)
            head = slice(at, at + 2 * DH)
            push(part.at[xx, :, 1 - c, :, head], rc.at[d, :, :, head], RC + 2 * d + half, sibling)

    halves = [slice(0, W), slice(W, 2 * W)]

    def core_sum(d, lo, hi, h):
        cs = halves[h]
        return part[(x + d) % 4, lo:hi, c, :, cs].astype(f32) + rc[d, lo:hi, :, cs].astype(f32)

    def x_first(d, h):
        cs = halves[h]
        arrived(rc.at[d, :, :, cs], RC + 2 * d + h)
        if d == 2:
            summed[2, :, :, cs] = core_sum(2, 0, NZ, h).astype(bf16)
            push(summed.at[2, 0:3, :, cs], ra.at[0, :, :, cs], RA + 2 * h, xr)
            push(summed.at[2, 3:6, :, cs], ra.at[1, :, :, cs], RA + 2 * h + 1, xl)
        elif d == 1:
            summed[1, 3:6, :, cs] = core_sum(1, 3, 6, h).astype(bf16)
            push(summed.at[1, 3:6, :, cs], rb.at[0, 3:6, :, cs], RB + 4 * h + 1, xr)
        else:
            summed[3, 0:3, :, cs] = core_sum(3, 0, 3, h).astype(bf16)
            push(summed.at[3, 0:3, :, cs], rb.at[1, 0:3, :, cs], RB + 4 * h + 2, xl)

    def x_second(h):
        cs = halves[h]
        arrived(ra.at[0, :, :, cs], RA + 2 * h)
        summed[1, 0:3, :, cs] = (core_sum(1, 0, 3, h) + ra[0, :, :, cs].astype(f32)).astype(bf16)
        push(summed.at[1, 0:3, :, cs], rb.at[0, 0:3, :, cs], RB + 4 * h, xr)
        arrived(ra.at[1, :, :, cs], RA + 2 * h + 1)
        summed[3, 3:6, :, cs] = (core_sum(3, 3, 6, h) + ra[1, :, :, cs].astype(f32)).astype(bf16)
        push(summed.at[3, 3:6, :, cs], rb.at[1, 3:6, :, cs], RB + 4 * h + 3, xl)

    def z_first(h):
        cs = halves[h]
        arrived(rc.at[0, :, :, cs], RC + h)
        arrived(rb.at[0, 3:6, :, cs], RB + 4 * h + 1)
        arrived(rb.at[1, 0:3, :, cs], RB + 4 * h + 2)
        arrived(rb.at[0, 0:3, :, cs], RB + 4 * h)
        arrived(rb.at[1, 3:6, :, cs], RB + 4 * h + 3)

        def x_sum(first, count):
            at = pl.ds(first, count)
            return (
                part[x, at, c, :, cs].astype(f32) + rc[0, at, :, cs].astype(f32)
            ) + (rb[0, at, :, cs].astype(f32) + rb[1, at, :, cs].astype(f32))

        zsend[0:2, :, cs] = x_sum(far_zh * 2, 2).astype(bf16)
        push(zsend.at[0:2, :, cs], rz.at[0:2, :, cs], RZ0 + h, partner)
        own_near[:, :, cs] = x_sum(near_zh * 2, 2)
        zsend[2:3, :, cs] = x_sum(zh * 2 + 1 - zl, 1).astype(bf16)
        push(zsend.at[2, :, cs], rz.at[2, :, cs], RZ1 + h, partner)
        gp_v[:, cs] = x_sum(z, 1)[0]

    def z_second(h):
        cs = halves[h]
        arrived(rz.at[0:2, :, cs], RZ0 + h)
        agg[:, :, cs] = (own_near[:, :, cs] + rz[0:2, :, cs].astype(f32)).astype(bf16)
        for i in range(2):
            push(agg.at[i, :, cs], rd.at[zl, :, cs], RD + 2 * h + zl, near[i])

    def z_third(h):
        cs = halves[h]
        arrived(rz.at[2, :, cs], RZ1 + h)
        arrived(rd.at[0, :, cs], RD + 2 * h)
        arrived(rd.at[1, :, cs], RD + 2 * h + 1)
        gp_v[:, cs] = (gp_v[:, cs] + rz[2, :, cs].astype(f32)) + (
            rd[0, :, cs].astype(f32) + rd[1, :, cs].astype(f32)
        )
        for g in (2 * h, 2 * h + 1):
            sl, at = slice(g * DH, (g + 1) * DH), 2 * g * DH
            outs.append(pltpu.make_async_copy(gp_v.at[:, at : at + DH], gpk_hbm.at[:, sl], osem.at[3 + 2 * g]))
            outs.append(pltpu.make_async_copy(gp_v.at[:, at + DH : at + 2 * DH], gpv_hbm.at[:, sl], osem.at[4 + 2 * g]))
        for copy in outs[-4:]:
            copy.start()

    def from_z(s):
        if s == 1:
            arrived(block(x, 1), Z0)
        elif s < 4:
            arrived(block(x, s), ZD + s - 2)
            push(block(x, s), block(x, s), ZR + s - 2, partner)
        else:
            arrived(block(x, s), ZR + s - 4)
        spread(s)

    loads[6].wait()
    loads[7].wait()
    own_tokens(0)
    own_tokens(1)
    from_z(1)
    own_tokens(2)
    own_tokens(3)
    outs = [
        pltpu.make_async_copy(gkr_v, gkr_hbm, osem.at[0]),
        pltpu.make_async_copy(gvr_v, gvr_hbm, osem.at[1]),
    ]
    for copy in outs:
        copy.start()
    from_z(2)
    from_z(3)
    hand_on(0)
    hand_on(1)
    from_z(4)
    from_z(5)
    hand_on(2)
    hand_on(3)
    last_of(0)
    last_of(1)
    work(0, 0)
    hand_on(4)
    hand_on(5)
    work(0, 1)
    last_of(2)
    last_of(3)
    work(1, 0)
    work(1, 1)
    last_of(4)
    last_of(5)
    work(3, 0)
    x_first(1, 0)
    work(3, 1)
    x_first(1, 1)
    work(2, 0)
    x_first(3, 0)
    work(2, 1)
    x_first(2, 0)
    x_first(3, 1)
    for g in range(HK):
        for r in range(R):
            sl = slice((g * R + r) * DH, (g * R + r + 1) * DH)
            gq_v[:, sl] = (gacc[g, :, r * RT : (r + 1) * RT].T * SCALE).astype(bf16)
    outs.append(pltpu.make_async_copy(gq_v, gq_hbm, osem.at[2]))
    outs[-1].start()
    x_first(2, 1)
    x_second(0)
    x_second(1)
    z_first(0)
    z_first(1)
    z_second(0)
    z_second(1)
    z_third(0)
    z_third(1)
    for copy in sends:
        copy.wait_send()
    for copy in outs:
        copy.wait()


NSEND = 100


def finish(*refs):
    ins, outs, held, sem = refs[:5], refs[5:10], refs[10:15], refs[15]
    pieces = [(1, slice(None)), (2, slice(None)), (3, slice(None)), (4, slice(None))]
    pieces += [(0, slice(i * 32, i * 32 + 32)) for i in range(4)]
    first, last = [], []
    for n, (i, at) in enumerate(pieces):
        first.append(pltpu.make_async_copy(ins[i].at[at], held[i].at[at], sem.at[n]))
        last.append(pltpu.make_async_copy(held[i].at[at], outs[i].at[at], sem.at[8 + n]))
        first[-1].start()
    for n in range(8):
        first[n].wait()
        last[n].start()
    for copy in last:
        copy.wait()


def shards(queries, resp_keys, resp_values, grad_out, forward_out, log_norm, prompt_keys, prompt_values, resp_len, seen_blocks):
    shape = jax.ShapeDtypeStruct
    results = [
        shape((RT, HQ * DH), bf16),
        shape((RT, W), bf16),
        shape((RT, W), bf16),
        shape((PB, W), f32),
        shape((PB, W), f32),
    ]
    any_space = pl.BlockSpec(memory_space=pl.ANY)
    vmem = pltpu.VMEM
    gq, gkr, gvr, gpk, gpv = pl.pallas_call(
        kernel,
        in_specs=[pl.BlockSpec(memory_space=pltpu.HBM)] * 2 + [any_space] * 8,
        out_specs=[any_space] * 5,
        out_shape=results,
        scratch_shapes=[
            vmem((RT, HQ * DH), bf16),
            vmem((RT, HQ * DH), bf16),
            vmem((RT, HQ * DH), bf16),
            vmem((HQ, 1, RT), f32),
            vmem((RT, W), bf16),
            vmem((RT, W), bf16),
            vmem((RT, HQ * DH), bf16),
            vmem((RT, W), bf16),
            vmem((RT, W), bf16),
            vmem((PB, 2 * W), f32),
            pltpu.SMEM((2, 1), jnp.int32),
            vmem((HK, R * RT, DH), bf16),
            vmem((HK, R * RT, DH), bf16),
            vmem((RT, DH), f32),
            vmem((2, DH, RT), f32),
            vmem((HK, DH, R * RT), f32),
            vmem((NX, NZ, 2, PB, 2 * W), bf16),
            vmem((NX, NZ, 2, PB, 2 * W), bf16),
            vmem((NX, NZ, PB, 2 * W), bf16),
            vmem((NX, NZ, PB, 2 * W), bf16),
            vmem((2, 3, PB, 2 * W), bf16),
            vmem((2, NZ, PB, 2 * W), bf16),
            vmem((3, PB, 2 * W), bf16),
            vmem((3, PB, 2 * W), bf16),
            vmem((2, PB, 2 * W), bf16),
            vmem((2, PB, 2 * W), bf16),
            vmem((2, PB, 2 * W), f32),
            pltpu.SemaphoreType.DMA((10,)),
            pltpu.SemaphoreType.DMA((11,)),
            pltpu.SemaphoreType.DMA((NSEND,)),
            pltpu.SemaphoreType.DMA((NSEM,)),
        ],
        compiler_params=pltpu.CompilerParams(collective_id=0, has_side_effects=True),
        name="attention_backward",
    )(
        resp_len, seen_blocks, queries[0], resp_keys[0], resp_values[0], grad_out[0], forward_out[0],
        log_norm.transpose(2, 0, 1), prompt_keys[0], prompt_values[0],
    )
    gq, gkr, gvr, gpk, gpv = pl.pallas_call(
        finish,
        in_specs=[any_space] * 5,
        out_specs=[any_space] * 5,
        out_shape=results,
        scratch_shapes=[vmem(r.shape, r.dtype) for r in results] + [pltpu.SemaphoreType.DMA((16,))],
        name="finish",
    )(gq, gkr, gvr, gpk, gpv)
    return gq[None], gkr[None], gvr[None], gpk[None], gpv[None]


def solution(mesh):
    rows = P(("dp", "resp"), None, None)
    prompt = P("resp", "dp", None)
    one = P(("dp", "resp"))
    return jax.shard_map(
        shards,
        mesh=mesh,
        in_specs=(rows,) * 6 + (prompt,) * 2 + (one,) * 2,
        out_specs=(rows,) * 3 + (prompt,) * 2,
        check_vma=False,
    )
```

time: 62.8 us -> 56.9 us (0.906)
  the two profiles are of different devices: /device:TPU:32 before, /device:TPU:34 now
where the time goes in v2:
time: 56.9 us; the launch traced here: 56.7 us
  Pallas kernels  54.8 us (96%)
  between operations  1.93 us (3%)
    pallas_call x1, Pallas kernels, shards(): pl.pallas_call(kernel, in_specs=[pl.BlockSpec(memory_space=pltpu.HBM)] *...  52.7 us
    pallas_call x1, Pallas kernels, shards(): pl.pallas_call(finish, in_specs=[any_space] * 5, out_specs=[any_space] *...  2.1 us

profile of v2, /device:TPU:34, one launch (start us, length us, event | category | flops | bytes accessed | tf_op | source)
XLA Modules:
  0.0 56.7 jit_solution(2277006708723447569)
XLA Ops:
  1.9 52.7 %attention_backward.1 = (bf16[128,2560]{1,0:T(8,128)(2,1)}, bf16[128,512]{1,0:T(8,128)(2,1)}, bf16[128,512]{1,0:T(8,128)(2,1)}, f32[16,512]{1,0:T(8,128)}, f32[16,512]{1,0:T(8,128)}) custom-call(s32[1]{0:T(128)S(6)} %copy.15.len_hbm, s32[1]{0:T(128)S(6)} %copy.16.seen_hbm, bf16[128,2560]{1,0:T(8,128)(2,1)} %bitcast.13, bf16[128,512]{1,0:T(8,128)(2,1)} %bitcast.16, ...), custom_call_target="tpu_custom_call" | custom-call | tf_op jit(solution)/shard_map/attention_backward/pallas_call | solution.py:367
  54.6 2.1 %finish.1 = (bf16[128,2560]{1,0:T(8,128)(2,1)}, bf16[128,512]{1,0:T(8,128)(2,1)}, bf16[128,512]{1,0:T(8,128)(2,1)}, f32[16,512]{1,0:T(8,128)}, f32[16,512]{1,0:T(8,128)}) custom-call(bf16[128,2560]{1,0:T(8,128)(2,1)} %get-tuple-element.15.refs_0_, bf16[128,512]{1,0:T(8,128)(2,1)} %get-tuple-element.16.refs_1_, bf16[128,512]{1,0:T(8,128)(2,1)} %get-tuple-element.17.refs_2_, ...), custom_call_target="tpu_custom_call" | custom-call | tf_op jit(solution)/shard_map/finish/pallas_call | solution.py:411

commit v3 on v2

--- a/solution.py
+++ b/solution.py
@@ -33,11 +33,11 @@
 
 def kernel(
     len_hbm, seen_hbm, q_hbm, kr_hbm, vr_hbm, do_hbm, fo_hbm, lse_hbm, pk_hbm, pv_hbm,
-    gq_hbm, gkr_hbm, gvr_hbm, gpk_hbm, gpv_hbm,
-    q_v, do_v, fo_v, lse_v, kr_v, vr_v, gq_v, gkr_v, gvr_v, gp_v,
+    gq_v, gkr_v, gvr_v, gpk_v, gpv_v,
+    q_v, do_v, fo_v, lse_v, kr_v, vr_v, gp_v,
     meta, qs, dos, col, rows, gacc,
     buf, part, rc, summed, ra, rb, zsend, rz, rd, agg, own_near,
-    lsem, osem, send, recv,
+    lsem, send, recv,
 ):
     dp, rs = lax.axis_index("dp"), lax.axis_index("resp")
     base = dp // 4 * 4
@@ -256,10 +256,8 @@
         )
         for g in (2 * h, 2 * h + 1):
             sl, at = slice(g * DH, (g + 1) * DH), 2 * g * DH
-            outs.append(pltpu.make_async_copy(gp_v.at[:, at : at + DH], gpk_hbm.at[:, sl], osem.at[3 + 2 * g]))
-            outs.append(pltpu.make_async_copy(gp_v.at[:, at + DH : at + 2 * DH], gpv_hbm.at[:, sl], osem.at[4 + 2 * g]))
-        for copy in outs[-4:]:
-            copy.start()
+            gpk_v[:, sl] = gp_v[:, at : at + DH]
+            gpv_v[:, sl] = gp_v[:, at + DH : at + 2 * DH]
 
     def from_z(s):
         if s == 1:
@@ -278,12 +276,6 @@
     from_z(1)
     own_tokens(2)
     own_tokens(3)
-    outs = [
-        pltpu.make_async_copy(gkr_v, gkr_hbm, osem.at[0]),
-        pltpu.make_async_copy(gvr_v, gvr_hbm, osem.at[1]),
-    ]
-    for copy in outs:
-        copy.start()
     from_z(2)
     from_z(3)
     hand_on(0)
@@ -297,28 +289,26 @@
     work(0, 0)
     hand_on(4)
     hand_on(5)
-    work(0, 1)
+    work(1, 0)
     last_of(2)
     last_of(3)
-    work(1, 0)
-    work(1, 1)
+    work(3, 0)
+    work(0, 1)
     last_of(4)
     last_of(5)
-    work(3, 0)
     x_first(1, 0)
+    work(1, 1)
+    x_first(3, 0)
+    work(2, 0)
+    x_first(1, 1)
     work(3, 1)
-    x_first(1, 1)
-    work(2, 0)
-    x_first(3, 0)
+    x_first(2, 0)
     work(2, 1)
-    x_first(2, 0)
     x_first(3, 1)
     for g in range(HK):
         for r in range(R):
             sl = slice((g * R + r) * DH, (g * R + r + 1) * DH)
             gq_v[:, sl] = (gacc[g, :, r * RT : (r + 1) * RT].T * SCALE).astype(bf16)
-    outs.append(pltpu.make_async_copy(gq_v, gq_hbm, osem.at[2]))
-    outs[-1].start()
     x_first(2, 1)
     x_second(0)
     x_second(1)
@@ -330,26 +320,17 @@
     z_third(1)
     for copy in sends:
         copy.wait_send()
-    for copy in outs:
-        copy.wait()
 
 
 NSEND = 100
 
 
 def finish(*refs):
-    ins, outs, held, sem = refs[:5], refs[5:10], refs[10:15], refs[15]
-    pieces = [(1, slice(None)), (2, slice(None)), (3, slice(None)), (4, slice(None))]
-    pieces += [(0, slice(i * 32, i * 32 + 32)) for i in range(4)]
-    first, last = [], []
-    for n, (i, at) in enumerate(pieces):
-        first.append(pltpu.make_async_copy(ins[i].at[at], held[i].at[at], sem.at[n]))
-        last.append(pltpu.make_async_copy(held[i].at[at], outs[i].at[at], sem.at[8 + n]))
-        first[-1].start()
-    for n in range(8):
-        first[n].wait()
-        last[n].start()
-    for copy in last:
+    sem = refs[10]
+    copies = [pltpu.make_async_copy(refs[i], refs[5 + i], sem.at[i]) for i in range(5)]
+    for copy in copies:
+        copy.start()
+    for copy in copies:
         copy.wait()
 
 
@@ -367,16 +348,13 @@
     gq, gkr, gvr, gpk, gpv = pl.pallas_call(
         kernel,
         in_specs=[pl.BlockSpec(memory_space=pltpu.HBM)] * 2 + [any_space] * 8,
-        out_specs=[any_space] * 5,
-        out_shape=results,
+        out_specs=[pl.BlockSpec(memory_space=pltpu.VMEM)] * 5,
+        out_shape=[vmem(r.shape, r.dtype) for r in results],
         scratch_shapes=[
             vmem((RT, HQ * DH), bf16),
             vmem((RT, HQ * DH), bf16),
             vmem((RT, HQ * DH), bf16),
             vmem((HQ, 1, RT), f32),
-            vmem((RT, W), bf16),
-            vmem((RT, W), bf16),
-            vmem((RT, HQ * DH), bf16),
             vmem((RT, W), bf16),
             vmem((RT, W), bf16),
             vmem((PB, 2 * W), f32),
@@ -398,7 +376,6 @@
             vmem((2, PB, 2 * W), bf16),
             vmem((2, PB, 2 * W), f32),
             pltpu.SemaphoreType.DMA((10,)),
-            pltpu.SemaphoreType.DMA((11,)),
             pltpu.SemaphoreType.DMA((NSEND,)),
             pltpu.SemaphoreType.DMA((NSEM,)),
         ],
@@ -413,9 +390,9 @@
         in_specs=[any_space] * 5,
         out_specs=[any_space] * 5,
         out_shape=results,
-        scratch_shapes=[vmem(r.shape, r.dtype) for r in results] + [pltpu.SemaphoreType.DMA((16,))],
+        scratch_shapes=[pltpu.SemaphoreType.DMA((5,))],
         name="finish",
-    )(gq, gkr, gvr, gpk, gpv)
+    )(*(pltpu.with_memory_space_constraint(r, pltpu.VMEM) for r in (gq, gkr, gvr, gpk, gpv)))
     return gq[None], gkr[None], gvr[None], gpk[None], gpv[None]
 
 

time: 56.9 us -> 54.6 us (0.960)
  the two profiles are of different devices: /device:TPU:34 before, /device:TPU:22 now
where the time goes in v3:
time: 54.6 us; the launch traced here: 54.4 us
  Pallas kernels  52.4 us (96%)
  between operations  1.93 us (4%)
    pallas_call x1, Pallas kernels, shards(): pl.pallas_call(kernel, in_specs=[pl.BlockSpec(memory_space=pltpu.HBM)] *...  51.5 us

profile of v3, /device:TPU:22, one launch (start us, length us, event | category | flops | bytes accessed | tf_op | source)
XLA Modules:
  0.0 54.4 jit_solution(10809629562843942663)
XLA Ops:
  1.9 51.5 %attention_backward.1 = (bf16[128,2560]{1,0:T(8,128)(2,1)S(1)}, bf16[128,512]{1,0:T(8,128)(2,1)S(1)}, bf16[128,512]{1,0:T(8,128)(2,1)S(1)}, f32[16,512]{1,0:T(8,128)S(1)}, f32[16,512]{1,0:T(8,128)S(1)}) custom-call(s32[1]{0:T(128)S(6)} %copy.15.len_hbm, s32[1]{0:T(128)S(6)} %copy.16.seen_hbm, bf16[128,2560]{1,0:T(8,128)(2,1)} %bitcast.13, ...), custom_call_target="tpu_custom_call" | custom-call | tf_op jit(solution)/shard_map/attention_backward/pallas_call | solution.py:348
  53.4 1.0 %finish.1 = (bf16[128,2560]{1,0:T(8,128)(2,1)}, bf16[128,512]{1,0:T(8,128)(2,1)}, bf16[128,512]{1,0:T(8,128)(2,1)}, f32[16,512]{1,0:T(8,128)}, f32[16,512]{1,0:T(8,128)}) custom-call(bf16[128,2560]{1,0:T(8,128)(2,1)S(1)} %get-tuple-element.15.refs_0_, bf16[128,512]{1,0:T(8,128)(2,1)S(1)} %get-tuple-element.16.refs_1_, ...), custom_call_target="tpu_custom_call" | custom-call | tf_op jit(solution)/shard_map/finish/pallas_call | solution.py:388

commit v4 on v3

--- a/solution.py
+++ b/solution.py
@@ -274,11 +274,11 @@
     own_tokens(0)
     own_tokens(1)
     from_z(1)
-    own_tokens(2)
-    own_tokens(3)
     from_z(2)
     from_z(3)
+    own_tokens(2)
     hand_on(0)
+    own_tokens(3)
     hand_on(1)
     from_z(4)
     from_z(5)
@@ -304,12 +304,12 @@
     work(3, 1)
     x_first(2, 0)
     work(2, 1)
-    x_first(3, 1)
     for g in range(HK):
         for r in range(R):
             sl = slice((g * R + r) * DH, (g * R + r + 1) * DH)
             gq_v[:, sl] = (gacc[g, :, r * RT : (r + 1) * RT].T * SCALE).astype(bf16)
     x_first(2, 1)
+    x_first(3, 1)
     x_second(0)
     x_second(1)
     z_first(0)

time: 54.6 us -> 54.4 us (level)
  the two profiles are of different devices: /device:TPU:22 before, /device:TPU:48 now
where the time goes in v4:
time: 54.4 us; the launch traced here: 54.2 us
  Pallas kernels  52.3 us (96%)
  between operations  1.93 us (4%)
    pallas_call x1, Pallas kernels, shards(): pl.pallas_call(kernel, in_specs=[pl.BlockSpec(memory_space=pltpu.HBM)] *...  51.3 us

profile of v4, /device:TPU:48, one launch (start us, length us, event | category | flops | bytes accessed | tf_op | source)
XLA Modules:
  0.0 54.2 jit_solution(15486698516994356079)
XLA Ops:
  1.9 51.3 %attention_backward.1 = (bf16[128,2560]{1,0:T(8,128)(2,1)S(1)}, bf16[128,512]{1,0:T(8,128)(2,1)S(1)}, bf16[128,512]{1,0:T(8,128)(2,1)S(1)}, f32[16,512]{1,0:T(8,128)S(1)}, f32[16,512]{1,0:T(8,128)S(1)}) custom-call(s32[1]{0:T(128)S(6)} %copy.15.len_hbm, s32[1]{0:T(128)S(6)} %copy.16.seen_hbm, bf16[128,2560]{1,0:T(8,128)(2,1)} %bitcast.13, ...), custom_call_target="tpu_custom_call" | custom-call | tf_op jit(solution)/shard_map/attention_backward/pallas_call | solution.py:348
  53.2 1.0 %finish.1 = (bf16[128,2560]{1,0:T(8,128)(2,1)}, bf16[128,512]{1,0:T(8,128)(2,1)}, bf16[128,512]{1,0:T(8,128)(2,1)}, f32[16,512]{1,0:T(8,128)}, f32[16,512]{1,0:T(8,128)}) custom-call(bf16[128,2560]{1,0:T(8,128)(2,1)S(1)} %get-tuple-element.15.refs_0_, bf16[128,512]{1,0:T(8,128)(2,1)S(1)} %get-tuple-element.16.refs_1_, ...), custom_call_target="tpu_custom_call" | custom-call | tf_op jit(solution)/shard_map/finish/pallas_call | solution.py:388
